TPU v7x, 256 devices: a whole 4x4x8 slice. The times are simulated.
256 devices in a mesh: seq: 64 (over x_hi, z, y), tp: 4 (over x_lo, core).
Axes of the slice: x: 4 (x_hi: 2, x_lo: 2; x = x_hi * 2 + x_lo), y: 4, z: 8, core: 2. Of those that a mesh axis runs over, the one named last changes fastest.
Arguments:
- query_rows: bfloat16 [16384, 4096], P('seq', 'tp'), may hold values from -130 to 130
- key_rows: bfloat16 [16384, 4096], P('seq', 'tp'), may hold values from -8 to 8
- value_rows: bfloat16 [16384, 4096], P('seq', 'tp'), may hold values from -6 to 6
- cotangent: bfloat16 [16384, 4096], P('seq', 'tp'), may hold values from -6 to 6
- global_pos: int32 [256], P('seq'), may hold values from 0 to 16383, as said below
- partner_mask: int32 [1], replicated, may hold values from 1 to 63
- rand_block: int32 [1, 64], replicated, may hold values from 0 to 1
Outputs:
- attention: bfloat16 [16384, 4096], P('seq', 'tp')
- grad_queries: bfloat16 [16384, 4096], P('seq', 'tp')
- grad_keys: bfloat16 [16384, 4096], P('seq', 'tp')
- grad_values: bfloat16 [16384, 4096], P('seq', 'tp')
Inputs may be any that keep to these rules, and one draw needn't show every extreme that they name: `global_pos`: the tokens of run d (positions d * 256 onward) hold exactly 4 global positions; all are distinct and in increasing order.
All inputs are finite; a program needn't handle non-finite values.
Results may differ from a plain program's by a relative error of at most 0.011.
Values may be sent and summed in bfloat16 or wider, within the bound.
A program may use at most 128 MiB of HBM per device.

v0:
```python
import jax
import jax.numpy as jnp
from jax import lax
from jax.sharding import PartitionSpec as P

HEAD_DIM = 128
BLK = 128


def from_partner(shard, axis, bit):
    return lax.ppermute(shard, axis, [(i, i ^ 1 << bit) for i in range(lax.axis_size(axis))])


def with_halo(shard, sides, width):
    for axis, dim in sides:
        size, length = (lax.axis_size(axis), shard.shape[dim])
        up = [(i, (i + 1) % size) for i in range(size - 1)]
        down = [(j, i) for i, j in up]
        last = lax.slice_in_dim(shard, length - width, length, axis=dim)
        first = lax.slice_in_dim(shard, 0, width, axis=dim)
        before = lax.ppermute(last, axis, up)
        after = lax.ppermute(first, axis, down)
        shard = jnp.concatenate([before, shard, after], axis=dim)
    return shard


def joined(value, axis, join):
    pieces = jax.tree.map(lambda part: lax.all_gather(part, axis), value)
    head = jax.tree.map(lambda part: part[0], pieces)
    tail = jax.tree.map(lambda part: part[1:], pieces)
    total, _ = lax.scan(lambda total, piece: (join(total, piece), None), head, tail)
    return total


def passed_along(block, axis, distance):
    devices = range(lax.axis_size(axis))
    route = [(i - distance, i) for i in devices if i - distance in devices]
    return lax.ppermute(block, axis, route)


def attend(query_inputs, gathered_keys, gathered_values, usable, incoming_gradient):
    softmax_scale_factor = query_inputs.shape[-1] ** (-0.5)
    logit_scores = (
        jnp.einsum("crj,prj->rcp", query_inputs, gathered_keys, preferred_element_type=jnp.float32)
        * softmax_scale_factor
    )
    logit_scores = jnp.where(usable[None, None, :], logit_scores, -1e30)
    maxima = jnp.max(logit_scores, axis=2, keepdims=True)
    raised = jnp.exp(logit_scores - maxima)
    totals = jnp.sum(raised, axis=2, keepdims=True)
    chances = raised / totals
    attention_weight_rows = chances.astype(jnp.bfloat16)
    attention_output = jnp.einsum(
        "bxl,lby->xby", attention_weight_rows, gathered_values, preferred_element_type=jnp.float32
    ).astype(jnp.bfloat16)
    deltas = jnp.transpose(
        jnp.sum(
            incoming_gradient.astype(jnp.float32) * attention_output.astype(jnp.float32), axis=2
        )
    )[:, :, None]
    probability_gradient = jnp.einsum(
        "crj,prj->rcp", incoming_gradient, gathered_values, preferred_element_type=jnp.float32
    )
    scaled_scores = (chances * (probability_gradient - deltas) * softmax_scale_factor).astype(
        jnp.bfloat16
    )
    query_gradient_rows = jnp.einsum(
        "bxl,lby->xby", scaled_scores, gathered_keys, preferred_element_type=jnp.float32
    )
    key_gradient_rows = jnp.einsum(
        "cgi,gcx->icx", scaled_scores, query_inputs, preferred_element_type=jnp.float32
    )
    value_gradient_rows = jnp.einsum(
        "cgi,gcx->icx", attention_weight_rows, incoming_gradient, preferred_element_type=jnp.float32
    )
    return (attention_output, query_gradient_rows, key_gradient_rows, value_gradient_rows)


def merge_stats(first, second):
    maxima = jnp.maximum(first[0], second[0])
    totals = first[1] * jnp.exp(first[0] - maxima) + second[1] * jnp.exp(second[0] - maxima)
    return (maxima, totals)


def level_order(levels):
    return list(range(levels))


def send_blocks(parcel, partner_mask, levels):
    for bit_level in level_order(levels):
        swapped = from_partner(parcel, "seq", bit_level)
        selected = jnp.right_shift(partner_mask, bit_level) % 2 == 1
        parcel = jnp.where(selected[:, None, None], swapped, parcel)
    return parcel


def return_grads(parcel, partner_mask, levels):
    for bit_level in level_order(levels):
        swapped = from_partner(parcel.astype(jnp.bfloat16), "seq", bit_level).astype(parcel.dtype)
        selected = jnp.right_shift(partner_mask, bit_level) % 2 == 1
        parcel = jnp.where(selected[:, None, None], swapped, parcel)
    return parcel


def per_device(query_rows, key_rows, value_rows, cotangent, global_pos, partner_mask, rand_block):
    local_count, columns = query_rows.shape
    head_here = columns // HEAD_DIM
    block_here = local_count // BLK
    rounds_count = partner_mask.shape[0]
    global_here = global_pos.shape[0]
    shard_index = lax.axis_index("seq")
    shard_count = lax.axis_size("seq")
    levels = shard_count.bit_length() - 1
    local_pos = global_pos - shard_index * local_count
    global_query, global_key, global_value, global_cot = (
        lax.all_gather(query_rows[local_pos], "seq", axis=0, tiled=True),
        lax.all_gather(key_rows[local_pos], "seq", axis=0, tiled=True),
        lax.all_gather(value_rows[local_pos], "seq", axis=0, tiled=True),
        lax.all_gather(cotangent[local_pos], "seq", axis=0, tiled=True),
    )
    global_count = global_query.shape[0]
    key_value = jnp.concatenate([key_rows, value_rows], axis=1)
    extended = with_halo(key_value, (("seq", 0),), BLK)
    requester = jnp.bitwise_xor(shard_index, partner_mask)
    chosen = rand_block[jnp.arange(rounds_count, dtype=jnp.int32), requester]
    outgoing = jnp.stack([lax.dynamic_slice_in_dim(key_value, chosen[0] * BLK, BLK, 0)])
    incoming = send_blocks(outgoing, partner_mask, levels)
    random_rows = incoming.reshape(rounds_count * BLK, 2 * columns)
    shared_keys = jnp.concatenate([random_rows[:, :columns], global_key], axis=0)
    shared_values = jnp.concatenate([random_rows[:, columns:], global_value], axis=0)
    shared_count = shared_keys.shape[0]
    global_marks = jnp.any(
        jnp.arange(local_count, dtype=jnp.int32)[:, None] == local_pos[None, :], axis=1
    )
    sparse_cot = jnp.where(global_marks[:, None], jnp.zeros_like(cotangent), cotangent)
    first_block = shard_index * block_here
    last_block = shard_count * block_here - 1

    def block_step(carried, number):
        begin = number * BLK
        window = lax.dynamic_slice_in_dim(extended, begin, 3 * BLK, 0)
        gathered_keys = jnp.concatenate([window[:, :columns], shared_keys], axis=0).reshape(
            -1, head_here, HEAD_DIM
        )
        gathered_values = jnp.concatenate([window[:, columns:], shared_values], axis=0).reshape(
            -1, head_here, HEAD_DIM
        )
        global_block = first_block + number
        usable = jnp.concatenate(
            [
                jnp.full((BLK,), global_block > 0),
                jnp.ones((BLK,), bool),
                jnp.full((BLK,), global_block < last_block),
                jnp.ones((shared_count,), bool),
            ]
        )
        attention_output, query_gradient_rows, key_gradient_rows, value_gradient_rows = attend(
            lax.dynamic_slice_in_dim(query_rows, begin, BLK, 0).reshape(BLK, head_here, HEAD_DIM),
            gathered_keys,
            gathered_values,
            usable,
            lax.dynamic_slice_in_dim(sparse_cot, begin, BLK, 0).reshape(BLK, head_here, HEAD_DIM),
        )
        key_flat = key_gradient_rows.reshape(-1, columns)
        value_flat = value_gradient_rows.reshape(-1, columns)
        return (
            carried,
            (
                attention_output.reshape(BLK, columns),
                query_gradient_rows.reshape(BLK, columns),
                key_flat[: 3 * BLK],
                value_flat[: 3 * BLK],
                key_flat[3 * BLK :],
                value_flat[3 * BLK :],
            ),
        )

    unused = jnp.zeros((), jnp.float32)
    unused, (sparse_out, sparse_dq, window_dk, window_dv, shared_dk, shared_dv) = lax.scan(
        block_step, unused, jnp.arange(block_here, dtype=jnp.int32)
    )
    sparse_out = sparse_out.reshape(local_count, columns)
    sparse_dq = sparse_dq.reshape(local_count, columns)
    ext_keys = jnp.zeros((local_count + 2 * BLK, columns), jnp.float32)
    ext_values = jnp.zeros((local_count + 2 * BLK, columns), jnp.float32)
    for block_number in range(block_here):
        lower = block_number * BLK
        ext_keys = ext_keys.at[lower : lower + 3 * BLK].add(window_dk[block_number])
        ext_values = ext_values.at[lower : lower + 3 * BLK].add(window_dv[block_number])
    grad_ext = jnp.concatenate([ext_keys, ext_values], axis=1)
    grad_shared = jnp.concatenate([jnp.sum(shared_dk, axis=0), jnp.sum(shared_dv, axis=0)], axis=1)
    softmax_scale_factor = HEAD_DIM ** (-0.5)
    query_per_head = global_query.reshape(global_count, head_here, HEAD_DIM)
    cotangent_head_rows = global_cot.reshape(global_count, head_here, HEAD_DIM)
    key_per_head = key_rows.reshape(local_count, head_here, HEAD_DIM)
    value_per_head = value_rows.reshape(local_count, head_here, HEAD_DIM)
    logit_scores = (
        jnp.einsum("crj,prj->rcp", query_per_head, key_per_head, preferred_element_type=jnp.float32)
        * softmax_scale_factor
    )
    local_max = jnp.max(logit_scores, axis=2)
    local_sum = jnp.sum(jnp.exp(logit_scores - local_max[:, :, None]), axis=2)
    maxima, totals = joined((local_max, local_sum), "seq", merge_stats)
    chances = jnp.exp(logit_scores - maxima[:, :, None]) / totals[:, :, None]
    attention_weight_rows = chances.astype(jnp.bfloat16)
    partial_out = jnp.einsum(
        "bxl,lby->xby", attention_weight_rows, value_per_head, preferred_element_type=jnp.float32
    ).reshape(global_count, columns)
    global_out = lax.psum(partial_out, "seq").astype(jnp.bfloat16)
    deltas = jnp.transpose(
        jnp.sum(
            cotangent_head_rows.astype(jnp.float32)
            * global_out.reshape(global_count, head_here, HEAD_DIM).astype(jnp.float32),
            axis=2,
        )
    )[:, :, None]
    probability_gradient = jnp.einsum(
        "crj,prj->rcp", cotangent_head_rows, value_per_head, preferred_element_type=jnp.float32
    )
    scaled_scores = (chances * (probability_gradient - deltas) * softmax_scale_factor).astype(
        jnp.bfloat16
    )
    global_dq = jnp.einsum(
        "bxl,lby->xby", scaled_scores, key_per_head, preferred_element_type=jnp.float32
    ).reshape(global_count, columns)
    local_dk = jnp.einsum(
        "cgi,gcx->icx", scaled_scores, query_per_head, preferred_element_type=jnp.float32
    ).reshape(local_count, columns)
    local_dv = jnp.einsum(
        "cgi,gcx->icx",
        attention_weight_rows,
        cotangent_head_rows,
        preferred_element_type=jnp.float32,
    ).reshape(local_count, columns)
    global_grads = jnp.concatenate([grad_shared[rounds_count * BLK :], global_dq], axis=1)
    summed = lax.psum(global_grads, "seq")
    owned_rows = lax.dynamic_slice_in_dim(summed, shard_index * global_here, global_here, 0)
    returned = return_grads(
        grad_shared[: rounds_count * BLK].reshape(rounds_count, BLK, 2 * columns),
        partner_mask,
        levels,
    )
    from_next = passed_along(grad_ext[:BLK].astype(jnp.bfloat16), "seq", -1).astype(jnp.float32)
    from_prev = passed_along(grad_ext[BLK + local_count :].astype(jnp.bfloat16), "seq", 1).astype(
        jnp.float32
    )
    own_grads = grad_ext[BLK : BLK + local_count]
    own_grads = own_grads.at[:BLK].add(from_prev).at[local_count - BLK :].add(from_next)
    landing = chosen[0] * BLK
    own_grads = lax.dynamic_update_slice_in_dim(
        own_grads, lax.dynamic_slice_in_dim(own_grads, landing, BLK, 0) + returned[0], landing, 0
    )
    own_grads = own_grads + jnp.concatenate([local_dk, local_dv], axis=1)
    own_grads = own_grads.at[local_pos].add(owned_rows[:, : 2 * columns])
    grad_query_rows = sparse_dq.at[local_pos].add(owned_rows[:, 2 * columns :])
    own_out = lax.dynamic_slice_in_dim(global_out, shard_index * global_here, global_here, 0)
    attention = sparse_out.at[local_pos].set(own_out)
    return (
        attention,
        grad_query_rows.astype(jnp.bfloat16),
        own_grads[:, :columns].astype(jnp.bfloat16),
        own_grads[:, columns:].astype(jnp.bfloat16),
    )


def solution(mesh):
    placed = (P("seq", "tp"), P("seq", "tp"), P("seq", "tp"), P("seq", "tp"), P("seq"), P(), P())
    return jax.shard_map(
        per_device,
        mesh=mesh,
        in_specs=placed,
        out_specs=(P("seq", "tp"), P("seq", "tp"), P("seq", "tp"), P("seq", "tp")),
        check_vma=False,
    )
```

profile of v0, /device:TPU:8, one launch (start us, length us, event | category | flops | bytes accessed | tf_op | source)
XLA Modules:
  0.0 2457.4 jit_solution(18070954303673704445)
XLA Ops:
  16.1 2.3 collective-permute-start.2
  18.4 2.5 collective-permute-start
  20.9 4.1 collective-permute-start.1
  26.8 185.5 %all-gather.8 = bf16[64,4,1024]{2,1,0:T(4,128)(2,1)S(1)} all-gather(bf16[1,4,1024]{2,1,0:T(4,128)(2,1)S(1)} %bitcast.219), channel_id=4, replica_groups=mesh['seq'=64,'tp'=4] {'seq'}, dimensions={0}, use_global_device_ids=true | all-gather | bytes 532480 | tf_op jit(solution)/shard_map/all_gather | solution.py:116
  213.7 183.7 %all-gather.4 = f32[512,256]{1,0:T(8,128)S(1)} all-gather(f32[8,256]{1,0:T(8,128)S(1)} %exponential_reduce_fusion), channel_id=6, replica_groups=mesh['seq'=64,'tp'=4] {'seq'}, dimensions={0}, use_global_device_ids=true | all-gather | bytes 532480 | tf_op jit(solution)/shard_map/all_gather | solution.py:28
  398.2 177.0 %all-gather.3 = f32[512,256]{1,0:T(8,128)S(1)} all-gather(f32[8,256]{1,0:T(8,128)S(1)} %get-tuple-element.345), channel_id=5, replica_groups=mesh['seq'=64,'tp'=4] {'seq'}, dimensions={0}, use_global_device_ids=true | all-gather | bytes 532480 | tf_op jit(solution)/shard_map/all_gather | solution.py:28
  576.0 47.3 %while.40 = (s32[]{:T(128)}, f32[8,256]{1,0:T(8,128)S(1)}, f32[8,256]{1,0:T(8,128)S(1)}, f32[63,8,256]{2,1,0:T(8,128)}, f32[63,8,256]{2,1,0:T(8,128)}, /*index=5*/s32[]{:T(128)}) while((s32[]{:T(128)}, f32[8,256]{1,0:T(8,128)S(1)}, f32[8,256]{1,0:T(8,128)S(1)}, f32[63,8,256]{2,1,0:T(8,128)}, f32[63,8,256]{2,1,0:T(8,128)}, ...), condition=%wide.region_9.10_spmd, body=%wide.region_8.9_spmd.sunk | while | flops 12290 | bytes 49225 | solution.py:31
  625.0 1.9 broadcast_select_fusion.1
  626.9 356.7 %all-reduce.6 = bf16[256,1024]{0,1:T(8,128)(2,1)S(1)} all-reduce(f32[256,1024]{0,1:T(8,128)} %bitcast.212), channel_id=1, replica_groups=mesh['seq'=64,'tp'=4] {'seq'}, use_global_device_ids=true, to_apply=%region_10.11 | all-reduce | flops 262144 | bytes 1572864 | tf_op jit(solution)/shard_map/psum | solution.py:209
  983.6 1.9 gather_fusion.3
  985.4 1.9 broadcast_select_fusion.2
  987.4 192.3 %all-gather.9 = bf16[64,4,1024]{2,1,0:T(4,128)(2,1)} all-gather(bf16[1,4,1024]{2,1,0:T(4,128)(2,1)S(1)} %bitcast.218), channel_id=7, replica_groups=mesh['seq'=64,'tp'=4] {'seq'}, dimensions={0}, use_global_device_ids=true | all-gather | bytes 532480 | tf_op jit(solution)/shard_map/all_gather | solution.py:119
  1186.7 190.3 %all-gather.6 = bf16[64,4,1024]{2,1,0:T(4,128)(2,1)} all-gather(bf16[1,4,1024]{2,1,0:T(4,128)(2,1)S(1)} %bitcast.217), channel_id=2, replica_groups=mesh['seq'=64,'tp'=4] {'seq'}, dimensions={0}, use_global_device_ids=true | all-gather | bytes 532480 | tf_op jit(solution)/shard_map/all_gather | solution.py:118
  1376.9 188.0 %all-gather.7 = bf16[64,4,1024]{2,1,0:T(4,128)(2,1)} all-gather(bf16[1,4,1024]{2,1,0:T(4,128)(2,1)S(1)} %bitcast.216), channel_id=3, replica_groups=mesh['seq'=64,'tp'=4] {'seq'}, dimensions={0}, use_global_device_ids=true | all-gather | bytes 532480 | tf_op jit(solution)/shard_map/all_gather | solution.py:117
  1568.2 19.4 collective-permute-done.5
  1588.5 2.0 copy.128
  1590.6 2.0 reshape.379
  1592.5 2.0 copy.130
  1595.5 2.0 copy.133
  1597.6 3.0 multiply_convert_fusion.1
  1600.5 4.2 collective-permute-done.6
  1605.8 3.1 collective-permute-start.7
  1609.8 2.8 pad_maximum_fusion.4
  1612.6 4.0 collective-permute-done.7
  1618.4 79.3 %while.39 = (s32[]{:T(128)}, bf16[2,128,1024]{2,1,0:T(8,128)(2,1)}, f32[2,128,1024]{2,1,0:T(8,128)}, f32[2,384,1024]{2,1,0:T(8,128)}, f32[2,384,1024]{2,1,0:T(8,...) while((s32[]{:T(128)}, bf16[2,128,1024]{2,1,0:T(8,128)(2,1)}, ...), condition=%wide.region_5.6_spmd, body=%wide.region_1.5_spmd.sunk | while | flops 1226704896 | bytes 130574560 | solution.py:179
  1622.6 1.9 constant_dynamic-slice_fusion.9
  1626.3 2.9 fusion.107
  1629.2 2.1 fusion.108
  1636.9 2.9 constant_dynamic-update-slice_fusion.15
  1644.3 2.0 fusion.110
  1646.2 3.0 copy.203
  1649.3 2.9 constant_dynamic-update-slice_fusion.14
  1662.2 1.9 constant_dynamic-slice_fusion.9
  1665.9 2.9 fusion.107
  1668.8 2.1 fusion.108
  1676.5 2.9 constant_dynamic-update-slice_fusion.15
  1683.9 2.0 fusion.110
  1685.9 3.0 copy.203
  1688.9 2.9 constant_dynamic-update-slice_fusion.14
  1697.6 2.3 reduce_sum.55
  1700.4 2.3 reduce_sum.56
  1704.3 2.1 convert_bitcast_fusion
  1706.4 2.6 collective-permute-start.10
  1710.5 2.6 copy.159
  1713.1 2.5 copy.160
  1715.6 2.5 fusion.52
  1718.1 2.6 copy.150
  1724.7 8.3 collective-permute-done.11
  1733.0 2.2 fusion.22
  1737.2 1.9 pad_maximum_fusion.3
  1739.2 5.5 collective-permute-done.12
  1746.5 3.0 fusion.15
  1749.9 11.7 collective-permute-done.13
  1762.6 2.8 collective-permute-start.14
  1766.4 2.0 collective-permute-start.8
  1770.1 4.7 collective-permute-start.9
  1774.8 2.5 scatter_fusion
  1777.3 3.7 collective-permute-done.14
  1783.0 2.1 fusion.19
  1785.1 2.5 fusion.20
  1787.6 5.5 collective-permute-done.15
  1793.2 2.7 fusion.21
  1795.9 1.9 maximum_add_fusion
  1797.8 647.4 %all-reduce.5.cloned.1.call-done = f32[256,3072]{1,0:T(8,128)} async-done(((f32[256,3072]{1,0:T(8,128)}), f32[256,3072]{1,0:T(8,128)}) %all-reduce.5.cloned.1.call-update) | async-done | bytes 3145744 | tf_op jit(solution)/shard_map/psum | solution.py:236
  (305 shorter events, 138.0 us)
Async XLA Ops:
  7.2 2438.1 %all-reduce.5.cloned.1.call-start = ((), (), s32[]{:S(2)}) async-start(), calls=%async_computation | async-start | bytes 6291456 | tf_op jit(solution)/shard_map/psum | solution.py:236
  11.7 1598.1 %copy-start.16 = (bf16[256,1024]{0,1:T(8,128)(2,1)}, bf16[256,1024]{0,1:T(8,128)(2,1)S(1)}, u32[]{:S(2)}) copy-start(bf16[256,1024]{0,1:T(8,128)(2,1)S(1)} %copy.125) | copy-start | bytes 1572868
  13.1 199.2 %copy-start.23 = (bf16[256,1024]{0,1:T(8,128)(2,1)}, bf16[256,1024]{0,1:T(8,128)(2,1)S(1)}, u32[]{:S(2)}) copy-start(bf16[256,1024]{0,1:T(8,128)(2,1)S(1)} %copy.126) | copy-start | bytes 1572868
  13.1 11.9 copy-start.43
  16.1 608.9 %collective-permute-start.2 = (bf16[1,128,2048]{2,1,0:T(8,128)(2,1)}, bf16[1,128,2048]{2,1,0:T(8,128)(2,1)}, u32[]{:S(2)}, u32[]{:S(2)}) collective-permute-start(bf16[1,128,2048]{2,1,0:T(8,128)(2,1)} %bitcast.27), channel_id=1, source_target_pairs={{0,4},{4,0},{8,12},{12,8},{16,20},{20,16},{24,28},{28,24},{32,36},... | collective-permute-start | bytes 1572872 | tf_op jit(solution)/shard_map/ppermute | solution.py:11
  18.4 1591.4 %collective-permute-start = (bf16[128,2048]{0,1:T(8,128)(2,1)}, bf16[128,2048]{0,1:T(8,128)(2,1)}, u32[]{:S(2)}, u32[]{:S(2)}) collective-permute-start(bf16[128,2048]{0,1:T(8,128)(2,1)} %get-tuple-element.341), channel_id=1, source_target_pairs={{0,4},{4,8},{8,12},{12,16},{16,20},{20,24},{24,28},{28,32},{32,36}... | collective-permute-start | bytes 1572872 | tf_op jit(solution)/shard_map/ppermute | solution.py:21
  20.9 1588.9 %collective-permute-start.1 = (bf16[128,2048]{0,1:T(8,128)(2,1)}, bf16[128,2048]{0,1:T(8,128)(2,1)}, u32[]{:S(2)}, u32[]{:S(2)}) collective-permute-start(bf16[128,2048]{0,1:T(8,128)(2,1)} %get-tuple-element.342), channel_id=1, source_target_pairs={{4,0},{8,4},{12,8},{16,12},{20,16},{24,20},{28,24},{32,28},{36,32}... | collective-permute-start | bytes 1572872 | tf_op jit(solution)/shard_map/ppermute | solution.py:22
  25.1 1.7 copy-start.41
  397.4 226.0 %copy-start.37 = (bf16[256,1024]{1,0:T(8,128)(2,1)S(1)}, bf16[256,1024]{1,0:T(8,128)(2,1)}, u32[]{:S(2)}) copy-start(bf16[256,1024]{1,0:T(8,128)(2,1)} %param.25) | copy-start | bytes 1572868
  626.9 358.6 %collective-permute-start.3 = (bf16[1,128,2048]{2,1,0:T(8,128)(2,1)}, bf16[1,128,2048]{2,1,0:T(8,128)(2,1)}, u32[]{:S(2)}, u32[]{:S(2)}) collective-permute-start(bf16[1,128,2048]{2,1,0:T(8,128)(2,1)} %broadcast_select_fusion.1), channel_id=1, source_target_pairs={{0,8},{4,12},{8,0},{12,4},{16,24},{20,28},{24,16},{28,20},{32,40},... | collective-permute-start | bytes 1572872 | tf_op jit(solution)/shard_map/ppermute | solution.py:11
  983.5 199.5 %copy-start.30 = (bf16[256,1024]{0,1:T(8,128)(2,1)}, bf16[256,1024]{0,1:T(8,128)(2,1)S(1)}, u32[]{:S(2)}) copy-start(bf16[256,1024]{0,1:T(8,128)(2,1)S(1)} %all-reduce.6) | copy-start | bytes 1572868
  987.3 577.6 %collective-permute-start.4 = (bf16[1,128,2048]{2,1,0:T(8,128)(2,1)}, bf16[1,128,2048]{2,1,0:T(8,128)(2,1)}, u32[]{:S(2)}, u32[]{:S(2)}) collective-permute-start(bf16[1,128,2048]{2,1,0:T(8,128)(2,1)} %broadcast_select_fusion.2), channel_id=1, source_target_pairs={{0,16},{4,20},{8,24},{12,28},{16,0},{20,4},{24,8},{28,12},{32,48},... | collective-permute-start | bytes 1572872 | tf_op jit(solution)/shard_map/ppermute | solution.py:11
  1186.7 379.5 %copy-start.26 = (f32[256,8,128]{2,1,0:T(8,128)S(1)}, f32[256,8,128]{2,1,0:T(8,128)}, u32[]{:S(2)}) copy-start(f32[256,8,128]{2,1,0:T(8,128)} %copy.145) | copy-start | bytes 3145732
  1186.7 379.9 %copy-start.38 = (bf16[256,8,128]{0,2,1:T(8,128)(2,1)S(1)}, bf16[256,8,128]{0,2,1:T(8,128)(2,1)}, u32[]{:S(2)}) copy-start(bf16[256,8,128]{0,2,1:T(8,128)(2,1)} %copy.157) | copy-start | bytes 1572868
  1566.1 21.4 collective-permute-start.5
  1587.5 7.0 copy-start.34
  1588.4 16.3 collective-permute-start.6
  1597.6 11.4 copy-start.35
  1600.5 9.3 copy-start.24
  1605.8 10.8 collective-permute-start.7
  1619.6 1.6 copy-start.11
  1619.6 1.7 copy-start.12
  1622.6 8.8 copy-start
  1625.6 3.6 copy-start.8
  1636.9 2.9 copy-start.2
  1636.9 4.1 copy-start.4
  1639.8 2.0 copy-start.1
  1641.8 1.9 copy-start.9
  1649.3 2.9 copy-start.3
  1654.8 2.3 copy-start.39
  1659.2 1.7 copy-start.12
  1662.2 8.8 copy-start
  1665.2 3.6 copy-start.8
  1676.5 3.0 copy-start.2
  1676.5 4.3 copy-start.4
  1679.5 2.0 copy-start.1
  1681.5 1.9 copy-start.9
  1688.9 2.9 copy-start.3
  1694.5 2.3 copy-start.39
  1704.3 4.8 copy-start.22
  1704.3 4.8 copy-start.25
  1706.4 14.6 collective-permute-start.10
  1710.5 5.1 copy-start.17
  1718.1 2.6 copy-start.31
  1722.2 2.4 copy-start.32
  1722.2 10.8 collective-permute-start.11
  1724.7 10.5 copy-start.15
  1733.0 2.2 copy-start.33
  1735.2 9.5 collective-permute-start.12
  1739.2 7.3 copy-start.5
  1746.3 15.2 copy-start.13
  1746.4 15.2 collective-permute-start.13
  1749.5 19.0 copy-start.6
  1761.6 4.8 copy-start.19
  1762.6 18.4 collective-permute-start.14
  1766.4 8.3 copy-start.42
  1766.4 14.6 copy-start.14
  1766.4 16.5 collective-permute-start.8
  1770.1 15.0 collective-permute-start.9
  1777.3 5.7 copy-start.7
  1782.4 10.8 collective-permute-start.15
  1785.1 8.1 copy-start.20
  1787.6 8.2 copy-start.27
  1787.6 8.2 copy-start.28
  (10 other events, 10.6 us)
Sparse Core Ops, SparseCore 0:
  1739.3 705.8 all-reduce.4
where the time goes:
time: 2470 us; the launch traced here: 2460 us
  blocking collectives  1470 us (60%)
  waiting for transfers between devices  710 us (29%)
  other arithmetic  102 us (4%)
  local copies, waits for them, and re-layouts  100 us (4%)
  matrix products  26.1 us (1%)
  starting transfers between devices  25.1 us (1%)
    psum x1, waiting for transfers between devices, per_device(): summed = lax.psum(global_grads, 'seq')  647 us
    all_gather x2, blocking collectives, joined(): pieces = jax.tree.map(lambda part: lax.all_gather(part, axis), value)  361 us
    psum x1, blocking collectives, per_device(): global_out = lax.psum(partial_out, 'seq').astype(jnp.bfloat16)  357 us
    all_gather x1, blocking collectives, per_device(): lax.all_gather(cotangent[local_pos], 'seq', axis=0, tiled=True)  192 us
    all_gather x1, blocking collectives, per_device(): lax.all_gather(value_rows[local_pos], 'seq', axis=0, tiled=True)  190 us
    all_gather x1, blocking collectives, per_device(): lax.all_gather(key_rows[local_pos], 'seq', axis=0, tiled=True)  188 us
    all_gather x1, blocking collectives, per_device(): lax.all_gather(query_rows[local_pos], 'seq', axis=0, tiled=True)  186 us
    ppermute x12, waiting for transfers between devices, from_partner(): lax.ppermute(shard, axis, [(i, i ^ 1 << bit) for i in range(lax.axis_size...  62.3 us
  transfers between devices with their start and end apart: 17, of which 9 were waited for; matrix products, arithmetic and copies ran while one was open for 5% of the time, Pallas kernels for 0%

commit v1 on v0

--- a/solution.py
+++ b/solution.py
@@ -112,10 +112,19 @@
     shard_count = lax.axis_size("seq")
     levels = shard_count.bit_length() - 1
     local_pos = global_pos - shard_index * local_count
+    arrange_knots_all = lambda mine_x: jnp.concatenate(
+        jax.lax.all_to_all(
+            jnp.stack([mine_x for _ in range(jax.lax.axis_size("seq"))]),
+            "seq",
+            split_axis=0,
+            concat_axis=0,
+        ),
+        axis=0,
+    )
     global_query, global_key, global_value, global_cot = (
         lax.all_gather(query_rows[local_pos], "seq", axis=0, tiled=True),
         lax.all_gather(key_rows[local_pos], "seq", axis=0, tiled=True),
-        lax.all_gather(value_rows[local_pos], "seq", axis=0, tiled=True),
+        arrange_knots_all(value_rows[local_pos]),
         lax.all_gather(cotangent[local_pos], "seq", axis=0, tiled=True),
     )
     global_count = global_query.shape[0]

time: 2470 us -> 2320 us (0.939)
  blocking collectives: 1470 us -> 1300 us
  starting transfers between devices: 25.1 us -> 59.6 us
    all_gather x1 -> x0, blocking collectives: 190 us -> none  [per_device(): lax.all_gather(value_rows[local_pos], 'seq', axis=0, tiled=True)]
  transfers between devices with their start and end apart: 17 -> 18, of which waited for: 9 -> 9; matrix products, arithmetic and copies ran while one was open for 5% -> 5% of each run, Pallas kernels for 0% -> 0%
where the time goes in v1:
time: 2320 us; the launch traced here: 2310 us
  blocking collectives  1300 us (56%)
  waiting for transfers between devices  704 us (30%)
  other arithmetic  101 us (4%)
  local copies, waits for them, and re-layouts  99.2 us (4%)
  starting transfers between devices  59.6 us (3%)
  matrix products  27.2 us (1%)
    psum x1, waiting for transfers between devices, per_device(): summed = lax.psum(global_grads, 'seq')  651 us
    all_gather x2, blocking collectives, joined(): pieces = jax.tree.map(lambda part: lax.all_gather(part, axis), value)  376 us
    psum x1, blocking collectives, per_device(): global_out = lax.psum(partial_out, 'seq').astype(jnp.bfloat16)  357 us
    all_gather x1, blocking collectives, per_device(): lax.all_gather(cotangent[local_pos], 'seq', axis=0, tiled=True)  193 us
    all_gather x1, blocking collectives, per_device(): lax.all_gather(key_rows[local_pos], 'seq', axis=0, tiled=True)  190 us
    all_gather x1, blocking collectives, per_device(): lax.all_gather(query_rows[local_pos], 'seq', axis=0, tiled=True)  182 us
    ppermute x12, waiting for transfers between devices, from_partner(): lax.ppermute(shard, axis, [(i, i ^ 1 << bit) for i in range(lax.axis_size...  53.1 us
  transfers between devices with their start and end apart: 18, of which 9 were waited for; matrix products, arithmetic and copies ran while one was open for 5% of the time, Pallas kernels for 0%

profile of v1, /device:TPU:8, one launch (start us, length us, event | category | flops | bytes accessed | tf_op | source)
XLA Modules:
  0.0 2310.3 jit_solution(17577260072753585162)
XLA Ops:
  16.1 2.3 collective-permute-start.2
  18.4 2.5 collective-permute-start
  20.8 4.2 collective-permute-start.1
  28.2 14.1 all-to-all-start
  44.0 182.0 %all-gather.6 = bf16[64,4,1024]{2,1,0:T(4,128)(2,1)S(1)} all-gather(bf16[1,4,1024]{2,1,0:T(4,128)(2,1)S(1)} %bitcast.217), channel_id=3, replica_groups=mesh['seq'=64,'tp'=4] {'seq'}, dimensions={0}, use_global_device_ids=true | all-gather | bytes 532480 | tf_op jit(solution)/shard_map/all_gather | solution.py:125
  227.1 189.6 %all-gather.2 = f32[512,256]{1,0:T(8,128)} all-gather(f32[8,256]{1,0:T(8,128)S(1)} %get-tuple-element.345), channel_id=4, replica_groups=mesh['seq'=64,'tp'=4] {'seq'}, dimensions={0}, use_global_device_ids=true | all-gather | bytes 532480 | tf_op jit(solution)/shard_map/all_gather | solution.py:28
  417.0 186.6 %all-gather.3 = f32[512,256]{1,0:T(8,128)} all-gather(f32[8,256]{1,0:T(8,128)S(1)} %exponential_reduce_fusion), channel_id=5, replica_groups=mesh['seq'=64,'tp'=4] {'seq'}, dimensions={0}, use_global_device_ids=true | all-gather | bytes 532480 | tf_op jit(solution)/shard_map/all_gather | solution.py:28
  603.6 1.9 slice_bitcast_fusion.2
  605.5 1.9 slice_bitcast_fusion.3
  608.6 47.1 %while.40 = (s32[]{:T(128)}, f32[8,256]{1,0:T(8,128)S(1)}, f32[8,256]{1,0:T(8,128)S(1)}, f32[63,8,256]{2,1,0:T(8,128)}, f32[63,8,256]{2,1,0:T(8,128)}, /*index=5*/s32[]{:T(128)}) while((s32[]{:T(128)}, f32[8,256]{1,0:T(8,128)S(1)}, f32[8,256]{1,0:T(8,128)S(1)}, f32[63,8,256]{2,1,0:T(8,128)}, f32[63,8,256]{2,1,0:T(8,128)}, ...), condition=%wide.region_9.10_spmd, body=%wide.region_8.9_spmd.sunk | while | flops 12290 | bytes 49225 | solution.py:31
  655.7 2.7 fusion.27
  659.2 356.8 %all-reduce.6 = bf16[256,1024]{0,1:T(8,128)(2,1)S(1)} all-reduce(f32[256,1024]{0,1:T(8,128)} %bitcast.211), channel_id=1, replica_groups=mesh['seq'=64,'tp'=4] {'seq'}, use_global_device_ids=true, to_apply=%region_10.11 | all-reduce | flops 262144 | bytes 1572864 | tf_op jit(solution)/shard_map/psum | solution.py:218
  1016.0 1.9 gather_fusion.1
  1020.8 192.7 %all-gather.7 = bf16[64,4,1024]{2,1,0:T(4,128)(2,1)} all-gather(bf16[1,4,1024]{2,1,0:T(4,128)(2,1)S(1)} %bitcast.216), channel_id=6, replica_groups=mesh['seq'=64,'tp'=4] {'seq'}, dimensions={0}, use_global_device_ids=true | all-gather | bytes 532480 | tf_op jit(solution)/shard_map/all_gather | solution.py:128
  1214.7 190.3 %all-gather.5 = bf16[64,4,1024]{2,1,0:T(4,128)(2,1)} all-gather(bf16[1,4,1024]{2,1,0:T(4,128)(2,1)S(1)} %bitcast.215), channel_id=2, replica_groups=mesh['seq'=64,'tp'=4] {'seq'}, dimensions={0}, use_global_device_ids=true | all-gather | bytes 532480 | tf_op jit(solution)/shard_map/all_gather | solution.py:126
  1405.0 1.9 broadcast_select_fusion.3
  1408.5 3.0 multiply_convert_fusion.1
  1411.5 12.9 collective-permute-done.5
  1424.4 1.9 broadcast_select_fusion.4
  1426.3 6.3 collective-permute-start.6
  1436.7 9.5 collective-permute-done.6
  1447.3 13.6 collective-permute-start.7
  1461.8 2.8 pad_maximum_fusion.4
  1469.9 79.0 %while.39 = (s32[]{:T(128)}, bf16[2,128,1024]{2,1,0:T(8,128)(2,1)}, f32[2,128,1024]{2,1,0:T(8,128)}, f32[2,384,1024]{2,1,0:T(8,128)}, f32[2,384,1024]{2,1,0:T(8,...) while((s32[]{:T(128)}, bf16[2,128,1024]{2,1,0:T(8,128)(2,1)}, ...), condition=%wide.region_5.6_spmd, body=%wide.region_1.5_spmd.sunk | while | flops 1226704896 | bytes 130574560 | solution.py:188
  1474.0 1.9 constant_dynamic-slice_fusion.9
  1477.7 2.9 fusion.107
  1480.6 2.1 fusion.108
  1488.2 2.9 constant_dynamic-update-slice_fusion.15
  1493.2 1.8 multiply_convert_fusion.3
  1495.6 2.0 fusion.110
  1497.6 3.1 copy.203
  1500.7 2.9 constant_dynamic-update-slice_fusion.14
  1513.5 1.9 constant_dynamic-slice_fusion.9
  1517.2 2.9 fusion.107
  1520.0 2.1 fusion.108
  1527.7 2.9 constant_dynamic-update-slice_fusion.15
  1532.7 1.8 multiply_convert_fusion.3
  1535.1 2.0 fusion.110
  1537.1 3.1 copy.203
  1540.2 2.9 constant_dynamic-update-slice_fusion.14
  1548.9 2.3 reduce_sum.55
  1551.6 2.3 reduce_sum.56
  1555.5 2.1 convert_bitcast_fusion
  1559.3 2.6 copy.159
  1562.0 2.5 copy.160
  1564.5 2.5 fusion.52
  1567.0 2.6 copy.150
  1573.6 8.3 collective-permute-done.11
  1581.9 2.2 fusion.22
  1586.1 1.9 pad_maximum_fusion.3
  1588.1 5.5 collective-permute-done.12
  1595.4 3.0 fusion.15
  1598.7 11.7 collective-permute-done.13
  1611.5 5.4 collective-permute-start.14
  1617.9 2.0 collective-permute-start.8
  1621.5 5.5 collective-permute-start.9
  1627.0 2.5 scatter_fusion
  1632.0 3.4 collective-permute-start.15
  1635.3 2.1 fusion.19
  1637.5 2.5 fusion.20
  1640.0 2.8 collective-permute-done.15
  1642.7 2.7 fusion.21
  1645.4 1.9 maximum_add_fusion
  1647.3 650.7 %all-reduce.5.cloned.1.call-done = f32[256,3072]{1,0:T(8,128)} async-done(((f32[256,3072]{1,0:T(8,128)}), f32[256,3072]{1,0:T(8,128)}) %all-reduce.5.cloned.1.call-update) | async-done | bytes 3145744 | tf_op jit(solution)/shard_map/psum | solution.py:245
  (305 shorter events, 138.0 us)
Async XLA Ops:
  11.6 1450.1 %copy-start.16 = (bf16[256,1024]{0,1:T(8,128)(2,1)}, bf16[256,1024]{0,1:T(8,128)(2,1)S(1)}, u32[]{:S(2)}) copy-start(bf16[256,1024]{0,1:T(8,128)(2,1)S(1)} %copy.125) | copy-start | bytes 1572868
  13.1 15.2 copy-start.23
  13.1 11.9 copy-start.41
  16.1 591.3 %collective-permute-start.2 = (bf16[1,128,2048]{2,1,0:T(8,128)(2,1)}, bf16[1,128,2048]{2,1,0:T(8,128)(2,1)}, u32[]{:S(2)}, u32[]{:S(2)}) collective-permute-start(bf16[1,128,2048]{2,1,0:T(8,128)(2,1)} %bitcast.27), channel_id=1, source_target_pairs={{0,4},{4,0},{8,12},{12,8},{16,20},{20,16},{24,28},{28,24},{32,36},... | collective-permute-start | bytes 1572872 | tf_op jit(solution)/shard_map/ppermute | solution.py:11
  18.4 1443.4 %collective-permute-start = (bf16[128,2048]{0,1:T(8,128)(2,1)}, bf16[128,2048]{0,1:T(8,128)(2,1)}, u32[]{:S(2)}, u32[]{:S(2)}) collective-permute-start(bf16[128,2048]{0,1:T(8,128)(2,1)} %get-tuple-element.341), channel_id=1, source_target_pairs={{0,4},{4,8},{8,12},{12,16},{16,20},{20,24},{24,28},{28,32},{32,36}... | collective-permute-start | bytes 1572872 | tf_op jit(solution)/shard_map/ppermute | solution.py:21
  20.8 1440.9 %collective-permute-start.1 = (bf16[128,2048]{0,1:T(8,128)(2,1)}, bf16[128,2048]{0,1:T(8,128)(2,1)}, u32[]{:S(2)}, u32[]{:S(2)}) collective-permute-start(bf16[128,2048]{0,1:T(8,128)(2,1)} %get-tuple-element.342), channel_id=1, source_target_pairs={{4,0},{8,4},{12,8},{16,12},{20,16},{24,20},{28,24},{32,28},{36,32}... | collective-permute-start | bytes 1572872 | tf_op jit(solution)/shard_map/ppermute | solution.py:22
  28.2 1436.3 %all-to-all-start = ((bf16[64,4,1024]{2,1,0:T(4,128)(2,1)}), bf16[64,4,1024]{2,1,0:T(4,128)(2,1)}, u32[]{:S(2)}, u32[]{:S(2)}) async-start(bf16[64,4,1024]{2,1,0:T(4,128)(2,1)} %stack.5), calls=%async_computation | async-start | bytes 1048576 | tf_op jit(solution)/shard_map/all_to_all | solution.py:116
  42.3 2255.8 %all-reduce.5.cloned.1.call-start = ((), (), s32[]{:S(2)}) async-start(), calls=%async_computation.1 | async-start | bytes 6291456 | tf_op jit(solution)/shard_map/psum | solution.py:245
  226.5 190.5 %copy-start.21 = (bf16[256,8,128]{0,2,1:T(8,128)(2,1)}, bf16[256,8,128]{0,2,1:T(8,128)(2,1)S(1)}, u32[]{:S(2)}) copy-start(bf16[256,8,128]{0,2,1:T(8,128)(2,1)S(1)} %copy.155) | copy-start | bytes 1572868
  417.0 191.5 %slice-start = ((f32[512,256]{1,0:T(8,128)}), f32[8,256]{1,0:T(8,128)S(1)}, s32[]{:S(2)}) async-start(f32[512,256]{1,0:T(8,128)} %all-gather.2), calls=%async_computation.2 | async-start | bytes 16384 | tf_op jit(solution)/shard_map/slice | solution.py:29
  603.6 5.0 slice-start.1
  608.4 49.9 %collective-permute-start.3 = (bf16[1,128,2048]{2,1,0:T(8,128)(2,1)S(1)}, bf16[1,128,2048]{2,1,0:T(8,128)(2,1)}, u32[]{:S(2)}, u32[]{:S(2)}) collective-permute-start(bf16[1,128,2048]{2,1,0:T(8,128)(2,1)S(1)} %broadcast_select_fusion.1), channel_id=1, source_target_pairs={{0,8},{4,12},{8,0},{12,4},{16,24},{20,28},{24,16},{28,20},{32,40},... | collective-permute-start | bytes 1572872 | tf_op jit(solution)/shard_map/ppermute | solution.py:11
  659.2 745.8 %collective-permute-start.4 = (bf16[1,128,2048]{2,1,0:T(8,128)(2,1)}, bf16[1,128,2048]{2,1,0:T(8,128)(2,1)}, u32[]{:S(2)}, u32[]{:S(2)}) collective-permute-start(bf16[1,128,2048]{2,1,0:T(8,128)(2,1)} %broadcast_select_fusion.2), channel_id=1, source_target_pairs={{0,16},{4,20},{8,24},{12,28},{16,0},{20,4},{24,8},{28,12},{32,48},... | collective-permute-start | bytes 1572872 | tf_op jit(solution)/shard_map/ppermute | solution.py:11
  1016.0 4.8 copy-start.30
  1214.7 192.2 %copy-start.26 = (f32[256,8,128]{2,1,0:T(8,128)S(1)}, f32[256,8,128]{2,1,0:T(8,128)}, u32[]{:S(2)}) copy-start(f32[256,8,128]{2,1,0:T(8,128)} %copy.145) | copy-start | bytes 3145732
  1406.9 17.4 collective-permute-start.5
  1408.5 24.0 %copy-start.36 = (bf16[256,8,128]{0,2,1:T(8,128)(2,1)S(1)}, bf16[256,8,128]{0,2,1:T(8,128)(2,1)}, u32[]{:S(2)}) copy-start(bf16[256,8,128]{0,2,1:T(8,128)(2,1)} %copy.157) | copy-start | bytes 1572868
  1426.3 9.3 copy-start.34
  1426.3 19.9 collective-permute-start.6
  1435.7 26.0 %copy-start.24 = (bf16[256,1024]{0,1:T(8,128)(2,1)S(1)}, bf16[256,1024]{0,1:T(8,128)(2,1)}, u32[]{:S(2)}) copy-start(bf16[256,1024]{0,1:T(8,128)(2,1)} %copy-done.23) | copy-start | bytes 1572868
  1447.3 20.7 collective-permute-start.7
  1471.0 1.7 copy-start.12
  1474.0 8.7 copy-start
  1477.0 3.5 copy-start.8
  1488.2 2.9 copy-start.2
  1488.2 4.2 copy-start.4
  1491.1 2.0 copy-start.1
  1493.2 1.9 copy-start.9
  1500.7 2.9 copy-start.3
  1506.2 2.3 copy-start.37
  1510.5 1.7 copy-start.12
  1513.5 8.7 copy-start
  1516.5 3.5 copy-start.8
  1527.7 3.0 copy-start.2
  1527.7 4.3 copy-start.4
  1530.7 2.0 copy-start.1
  1532.7 1.9 copy-start.9
  1540.2 2.9 copy-start.3
  1545.7 2.3 copy-start.37
  1555.5 2.4 copy-start.22
  1555.5 2.4 copy-start.25
  1557.6 12.3 collective-permute-start.10
  1559.3 5.2 copy-start.17
  1567.0 2.6 copy-start.31
  1571.1 2.4 copy-start.32
  1571.1 10.8 collective-permute-start.11
  1573.6 10.5 copy-start.15
  1581.9 2.2 copy-start.33
  1584.1 9.5 collective-permute-start.12
  1588.1 7.3 copy-start.5
  1595.3 15.2 copy-start.13
  1595.3 15.2 collective-permute-start.13
  1598.4 21.6 copy-start.6
  1610.5 7.4 copy-start.19
  1611.5 19.1 collective-permute-start.14
  1617.9 9.1 copy-start.40
  1617.9 12.6 copy-start.14
  1617.9 17.4 collective-permute-start.8
  1621.5 15.9 collective-permute-start.9
  1629.5 5.8 copy-start.7
  1632.0 10.8 collective-permute-start.15
  1637.4 5.3 copy-start.20
  1640.0 5.5 copy-start.27
  1640.0 5.5 copy-start.28
  (11 other events, 11.9 us)
Sparse Core Ops, SparseCore 0:
  1588.2 709.8 all-reduce.4
